TPU v7x, 256 devices: a whole 4x4x8 slice. The times are simulated.
256 devices in a mesh: occ: 16 (over z, y_hi), aux: 16 (over y_lo, x, core).
Axes of the slice: x: 4, y: 4 (y_hi: 2, y_lo: 2; y = y_hi * 2 + y_lo), z: 8, core: 2. Of those that a mesh axis runs over, the one named last changes fastest.
Arguments:
- orbital_b: bfloat16 [128, 3072, 768], P('occ', 'aux'), may hold values from -0.75 to 0.75
- occ_energy: float32 [128], replicated, may hold values from -3 to -0.5
- vir_energy: float32 [768], replicated, may hold values from 0.2 to 3
Outputs:
- gradient_term: bfloat16 [128, 3072, 768], P('occ', 'aux')
All inputs are finite; a program needn't handle non-finite values.
Results may differ from a plain program's by a relative error of at most 0.0044.
Values may be sent and summed in bfloat16 or wider, within the bound.
A program may use at most 64 MiB of HBM per device.

v0:
```python
import jax
import jax.numpy as jnp
from jax import lax
from jax.sharding import PartitionSpec as P


def shifted(value, axis, steps):
    count = lax.axis_size(axis)
    initial, last = (max(0, -steps), min(count, count - steps))
    return lax.ppermute(value, axis, [(source, source + steps) for source in range(initial, last)])


def shards(orbital_b, occ_energy, vir_energy):
    occ_index = lax.axis_index("occ")
    aux_index = lax.axis_index("aux")
    occ_count = lax.axis_size("occ")
    block_rows = orbital_b.shape[0]
    vir_width = orbital_b.shape[2]
    slab_width = vir_width // lax.axis_size("aux")
    columns = lax.all_to_all(orbital_b, "aux", split_axis=2, concat_axis=1, tiled=True)
    own_energy = lax.dynamic_slice_in_dim(occ_energy, occ_index * block_rows, block_rows)
    vir_slab = lax.dynamic_slice_in_dim(vir_energy, aux_index * slab_width, slab_width)
    energy_left = occ_energy[jnp.maximum(occ_index - 1, 0) * block_rows]
    energy_right = occ_energy[jnp.minimum(occ_index + 1, occ_count - 1) * block_rows]
    partner_energy = jnp.stack([energy_left, energy_right])
    leading = columns[:1]
    from_left_block = shifted(leading, "occ", 1)
    from_right_block = shifted(leading, "occ", -1)
    partners = jnp.concatenate([from_left_block, from_right_block], axis=0)
    segment = lax.all_gather(partners, "aux", axis=2, tiled=True)
    integral = jnp.einsum("iPa,pPb->iapb", columns, segment, preferred_element_type=jnp.float32)
    denominator = (
        vir_slab[None, :, None, None]
        + vir_energy[None, None, None, :]
        - own_energy[:, None, None, None]
        - partner_energy[None, None, :, None]
    )
    amplitude = (integral / denominator).astype(jnp.bfloat16)
    running = jnp.einsum("iapb,pPb->iPa", amplitude, segment, preferred_element_type=jnp.float32)
    gradient_slab = running.astype(jnp.bfloat16)
    return lax.all_to_all(gradient_slab, "aux", split_axis=1, concat_axis=2, tiled=True)


def solution(mesh):
    placed = (P("occ", "aux", None), P(), P())
    return jax.shard_map(
        shards, mesh=mesh, in_specs=placed, out_specs=P("occ", "aux", None), check_vma=False
    )
```

profile of v0, /device:TPU:1, one launch (start us, length us, event | category | flops | bytes accessed | tf_op | source)
XLA Modules:
  0.0 229.1 jit_solution(18051163929910925184)
XLA Ops:
  6.5 0.0 all-gather.2.cloned.1.call-start
  6.5 5.0 %copy.15 = bf16[8,192,768]{1,0,2:T(8,128)(2,1)} copy(bf16[8,192,768]{2,1,0:T(8,128)(2,1)} %param.3) | data formatting | bytes 4718592 | tf_op args[0]
  11.6 44.4 %all_to_all.36 = bf16[8,192,768]{1,0,2:T(8,128)(2,1)S(1)} all-to-all(bf16[8,192,768]{1,0,2:T(8,128)(2,1)} %copy.15), channel_id=1, replica_groups=mesh['occ'=16,'aux'=16] {'aux'}, dimensions={2} | all-to-all | bytes 4718592 | tf_op jit(solution)/shard_map/all_to_all | solution.py:20
  55.9 0.6 copy.16
  56.6 0.0 copy-start.1
  56.6 0.0 copy-start
  56.7 0.1 copy.17
  56.8 1.1 slice.7
  57.9 1.3 collective-permute-start.1
  59.2 5.5 %collective-permute-start = (bf16[1,3072,48]{1,2,0:T(8,128)(2,1)}, bf16[1,3072,48]{1,2,0:T(8,128)(2,1)S(1)}, u32[]{:S(2)}, u32[]{:S(2)}) collective-permute-start(bf16[1,3072,48]{1,2,0:T(8,128)(2,1)} %slice.7), channel_id=1, source_target_pairs={{0,16},{16,32},{32,48},{48,64},{64,80},{80,96},{96,112},{112,128},... | collective-permute-start | bytes 884744 | tf_op jit(solution)/shard_map/ppermute | solution.py:10
  64.7 3.9 %collective-permute-done.1 = bf16[1,3072,48]{1,2,0:T(8,128)(2,1)S(1)} collective-permute-done((bf16[1,3072,48]{1,2,0:T(8,128)(2,1)}, bf16[1,3072,48]{1,2,0:T(8,128)(2,1)S(1)}, u32[]{:S(2)}, u32[]{:S(2)}) %collective-permute-start.1) | collective-permute-done | bytes 294944 | tf_op jit(solution)/shard_map/ppermute | solution.py:10
  68.6 8.0 %collective-permute-done = bf16[1,3072,48]{1,2,0:T(8,128)(2,1)S(1)} collective-permute-done((bf16[1,3072,48]{1,2,0:T(8,128)(2,1)}, bf16[1,3072,48]{1,2,0:T(8,128)(2,1)S(1)}, u32[]{:S(2)}, u32[]{:S(2)}) %collective-permute-start) | collective-permute-done | bytes 294944 | tf_op jit(solution)/shard_map/ppermute | solution.py:10
  76.6 0.9 pad_maximum_fusion
  77.5 0.0 all-gather.2.cloned.1.call-update
  77.6 0.0 copy-done.1
  77.6 0.1 dynamic_slice.13
  77.7 0.0 copy-done
  77.7 0.1 dynamic_slice.12
  77.7 0.6 fusion.15
  78.4 1.3 pad_maximum_fusion.1
  79.7 0.1 broadcast_add_fusion
  79.8 1.2 broadcast_subtract_fusion
  81.0 3.4 %copy.18 = bf16[8,16,192,48]{2,1,3,0:T(8,128)(2,1)} copy(bf16[8,16,192,48]{2,0,3,1:T(8,128)(2,1)S(1)} %bitcast.46) | data formatting | bytes 4718592 | tf_op jit(solution)/shard_map/all_to_all | solution.py:20
  84.4 5.1 %reshape.41 = bf16[8,3072,48,1]{1,2,0,3:T(8,128)(2,1)S(1)} reshape(bf16[8,16,192,48]{2,1,3,0:T(8,128)(2,1)} %copy.18) | data formatting | bytes 4718592 | tf_op jit(solution)/shard_map/all_to_all | solution.py:20
  89.5 50.5 %all-gather.2.cloned.1.call-done = bf16[2,3072,768]{1,2,0:T(8,128)(2,1)} async-done(((bf16[2,3072,48]{1,2,0:T(8,128)(2,1)}), bf16[2,3072,768]{1,2,0:T(8,128)(2,1)}) %all-gather.2.cloned.1.call-update) | async-done | bytes 9437200 | tf_op jit(solution)/shard_map/all_gather | solution.py:30
  140.0 0.0 copy-start.2
  140.0 8.0 %fusion.9 = bf16[8,48,2,768]{3,1,2,0:T(8,128)(2,1)S(1)} fusion(bf16[8,3072,48,1]{1,2,0,3:T(8,128)(2,1)S(1)} %reshape.41, bf16[2,3072,768]{1,2,0:T(8,128)(2,1)} %all-gather.2.cloned.1.call-done, f32[2]{0:T(128)S(1)} %pad_maximum_fusion.1, f32[8,48,768]{2,1,0:T(8,128)} %broadcast_subtract_fusion), kind=kOutput, calls=%fused_computation.7 | convolution fusion | flops 3625648128 | bytes 14155784 | tf_op jit(solution)/shard_map/iPa,pPb->iapb/dot_general | solution.py:31
  147.9 0.0 copy-done.2
  148.0 4.2 %fusion.6 = bf16[8,3072,48]{1,2,0:T(8,128)(2,1)S(1)} fusion(bf16[8,48,2,768]{3,1,2,0:T(8,128)(2,1)S(1)} %fusion.9, bf16[2,3072,768]{1,2,0:T(8,128)(2,1)S(1)} %copy-done.2), kind=kOutput, calls=%fused_computation.5 | convolution fusion | flops 3625058304 | bytes 12976128 | tf_op jit(solution)/shard_map/iapb,pPb->iPa/dot_general | solution.py:39
  152.1 6.0 %copy.19 = bf16[8,3072,48]{2,0,1:T(8,128)(2,1)} copy(bf16[8,3072,48]{1,2,0:T(8,128)(2,1)S(1)} %fusion.6) | data formatting | bytes 4718592 | tf_op jit(solution)/shard_map/convert_element_type | solution.py:40
  158.1 10.3 %reshape.44 = bf16[16,2,36864]{2,1,0:T(2,128)(2,1)S(1)} reshape(bf16[3072,8,48]{2,1,0:T(8,128)(2,1)} %bitcast.48) | data formatting | bytes 4718592
  168.4 34.7 %all_to_all.37 = bf16[16,2,36864]{2,1,0:T(2,128)(2,1)} all-to-all(bf16[16,2,36864]{2,1,0:T(2,128)(2,1)S(1)} %reshape.44), channel_id=1, replica_groups=mesh['occ'=16,'aux'=16] {'aux'}, dimensions={0} | all-to-all | bytes 4718592 | tf_op jit(solution)/shard_map/all_to_all | solution.py:41
  203.2 9.2 %reshape.45 = bf16[3072,8,48]{2,1,0:T(8,128)(2,1)} reshape(bf16[16,2,36864]{2,1,0:T(2,128)(2,1)} %all_to_all.37) | data formatting | bytes 4718592
  212.4 7.2 %copy.20 = bf16[8,16,192,48]{2,3,1,0:T(8,128)(2,1)S(1)} copy(bf16[8,16,192,48]{3,0,2,1:T(8,128)(2,1)} %bitcast.47) | data formatting | bytes 4718592 | tf_op jit(solution)/shard_map/all_to_all | solution.py:41
  219.6 2.6 %copy.21 = bf16[8,192,768]{2,1,0:T(8,128)(2,1)} copy(bf16[8,192,768]{1,2,0:T(8,128)(2,1)S(1)} %bitcast.49) | data formatting | bytes 4718592 | tf_op jit(solution)/shard_map/all_to_all | solution.py:41
  (1 shorter events, 0.0 us)
Async XLA Ops:
  6.5 133.4 %all-gather.2.cloned.1.call-start = ((), (), s32[]{:S(2)}) async-start(), calls=%async_computation.2 | async-start | bytes 10027008 | tf_op jit(solution)/shard_map/all_gather | solution.py:30
  56.6 21.0 %copy-start.1 = (f32[128]{0:T(128)S(1)}, f32[128]{0:T(128)}, u32[]{:S(2)}) copy-start(f32[128]{0:T(128)} %param.4) | copy-start | bytes 1540
  56.6 21.0 %copy-start = (f32[768]{0:T(1024)S(1)}, f32[768]{0:T(1024)}, u32[]{:S(2)}) copy-start(f32[768]{0:T(1024)} %param.5) | copy-start | bytes 9220
  57.9 10.7 %collective-permute-start.1 = (bf16[1,3072,48]{1,2,0:T(8,128)(2,1)}, bf16[1,3072,48]{1,2,0:T(8,128)(2,1)S(1)}, u32[]{:S(2)}, u32[]{:S(2)}) collective-permute-start(bf16[1,3072,48]{1,2,0:T(8,128)(2,1)} %slice.7), channel_id=1, source_target_pairs={{16,0},{32,16},{48,32},{64,48},{80,64},{96,80},{112,96},{128,112},... | collective-permute-start | bytes 884744 | tf_op jit(solution)/shard_map/ppermute | solution.py:10
  59.2 17.5 %collective-permute-start = (bf16[1,3072,48]{1,2,0:T(8,128)(2,1)}, bf16[1,3072,48]{1,2,0:T(8,128)(2,1)S(1)}, u32[]{:S(2)}, u32[]{:S(2)}) collective-permute-start(bf16[1,3072,48]{1,2,0:T(8,128)(2,1)} %slice.7), channel_id=1, source_target_pairs={{0,16},{16,32},{32,48},{48,64},{64,80},{80,96},{96,112},{112,128},... | collective-permute-start | bytes 884744 | tf_op jit(solution)/shard_map/ppermute | solution.py:10
  140.0 8.0 %copy-start.2 = (bf16[2,3072,768]{1,2,0:T(8,128)(2,1)S(1)}, bf16[2,3072,768]{1,2,0:T(8,128)(2,1)}, u32[]{:S(2)}) copy-start(bf16[2,3072,768]{1,2,0:T(8,128)(2,1)} %all-gather.2.cloned.1.call-done) | copy-start | bytes 28311556
Sparse Core Ops, SparseCore 0:
  77.7 62.2 all-gather.1
where the time goes:
time: 230 us; the launch traced here: 229 us
  blocking collectives  79.1 us (34%)
  waiting for transfers between devices  62.5 us (27%)
  local copies, waits for them, and re-layouts  51.5 us (22%)
  between operations  13.5 us (6%)
  matrix products  12.1 us (5%)
  starting transfers between devices  6.79 us (3%)
  other arithmetic  3.49 us (2%)
    all_gather x1, waiting for transfers between devices, shards(): segment = lax.all_gather(partners, 'aux', axis=2, tiled=True)  50.5 us
    all_to_all x1, blocking collectives, shards(): lax.all_to_all(orbital_b, 'aux', split_axis=2, concat_axis=1, tiled=True)  44.4 us
    all_to_all x1, blocking collectives, shards(): lax.all_to_all(gradient_slab, 'aux', split_axis=1, concat_axis=2, tiled=T...  34.7 us
    unnamed x9, local copies, waits for them, and re-layouts  24.6 us
    ppermute x2, waiting for transfers between devices, shifted(): lax.ppermute(value, axis, [(source, source + steps) for source in range(i...  12 us
    all_to_all x2, local copies, waits for them, and re-layouts, shards(): lax.all_to_all(gradient_slab, 'aux', split_axis=1, concat_axis=2, tiled=T...  9.8 us
    all_to_all x3, local copies, waits for them, and re-layouts, shards(): lax.all_to_all(orbital_b, 'aux', split_axis=2, concat_axis=1, tiled=True)  9.12 us
    dot_general x1, matrix products, shards(): jnp.einsum('iPa,pPb->iapb', columns, segment, preferred_element_type=jnp....  7.96 us
  transfers between devices with their start and end apart: 3, of which 3 were waited for; matrix products, arithmetic and copies ran while one was open for 5% of the time, Pallas kernels for 0%

commit v1 on v0

--- a/solution.py
+++ b/solution.py
@@ -2,6 +2,7 @@
 import jax.numpy as jnp
 from jax import lax
 from jax.sharding import PartitionSpec as P
+from jax.lax import all_to_all, axis_size
 
 
 def shifted(value, axis, steps):
@@ -27,7 +28,15 @@
     from_left_block = shifted(leading, "occ", 1)
     from_right_block = shifted(leading, "occ", -1)
     partners = jnp.concatenate([from_left_block, from_right_block], axis=0)
-    segment = lax.all_gather(partners, "aux", axis=2, tiled=True)
+    segment = jnp.concatenate(
+        all_to_all(
+            jnp.stack([partners] * axis_size("aux"), axis=0),
+            concat_axis=0,
+            axis_name="aux",
+            split_axis=0,
+        ),
+        axis=2,
+    )
     integral = jnp.einsum("iPa,pPb->iapb", columns, segment, preferred_element_type=jnp.float32)
     denominator = (
         vir_slab[None, :, None, None]

time: 230 us -> 300 us (1.30)
  waiting for transfers between devices: 62.5 us -> 126 us
  local copies, waits for them, and re-layouts: 51.5 us -> 65.1 us
  between operations: 13.5 us -> 0.11 us
  starting transfers between devices: 6.79 us -> 11.9 us
    all_to_all x0 -> x1, waiting for transfers between devices: none -> 114 us  [shards(): all_to_all(jnp.stack([partners] * axis_size('aux'), axis=0), concat_axis=...]
    all_gather x1 -> x0, waiting for transfers between devices: 50.5 us -> none  [shards(): segment = lax.all_gather(partners, 'aux', axis=2, tiled=True)]
    all_to_all x0 -> x1, local copies, waits for them, and re-layouts: none -> 8.71 us  [shards(): all_to_all(jnp.stack([partners] * axis_size('aux'), axis=0), concat_axis=...]
    all_to_all x0 -> x1, starting transfers between devices: none -> 5.14 us  [shards(): all_to_all(jnp.stack([partners] * axis_size('aux'), axis=0), concat_axis=...]
    another operation x0 -> x1, local copies, waits for them, and re-layouts: none -> 4.84 us  [shards(): jnp.stack([partners] * axis_size('aux'), axis=0)]
  transfers between devices with their start and end apart: 3 -> 3, of which waited for: 3 -> 3; matrix products, arithmetic and copies ran while one was open for 5% -> 4% of each run, Pallas kernels for 0% -> 0%
where the time goes in v1:
time: 300 us; the launch traced here: 297 us
  waiting for transfers between devices  126 us (42%)
  blocking collectives  79.4 us (26%)
  local copies, waits for them, and re-layouts  65.1 us (22%)
  matrix products  12.1 us (4%)
  starting transfers between devices  11.9 us (4%)
    all_to_all x1, waiting for transfers between devices, shards(): all_to_all(jnp.stack([partners] * axis_size('aux'), axis=0), concat_axis=...  114 us
    all_to_all x1, blocking collectives, shards(): lax.all_to_all(orbital_b, 'aux', split_axis=2, concat_axis=1, tiled=True)  44.4 us
    all_to_all x1, blocking collectives, shards(): lax.all_to_all(gradient_slab, 'aux', split_axis=1, concat_axis=2, tiled=T...  35 us
    unnamed x9, local copies, waits for them, and re-layouts  24.6 us
    ppermute x2, waiting for transfers between devices, shifted(): lax.ppermute(value, axis, [(source, source + steps) for source in range(i...  12 us
    all_to_all x2, local copies, waits for them, and re-layouts, shards(): lax.all_to_all(gradient_slab, 'aux', split_axis=1, concat_axis=2, tiled=T...  9.8 us
    all_to_all x3, local copies, waits for them, and re-layouts, shards(): lax.all_to_all(orbital_b, 'aux', split_axis=2, concat_axis=1, tiled=True)  9.14 us
    all_to_all x1, local copies, waits for them, and re-layouts, shards(): all_to_all(jnp.stack([partners] * axis_size('aux'), axis=0), concat_axis=...  8.71 us
  transfers between devices with their start and end apart: 3, of which 3 were waited for; matrix products, arithmetic and copies ran while one was open for 4% of the time, Pallas kernels for 0%

profile of v1, /device:TPU:1, one launch (start us, length us, event | category | flops | bytes accessed | tf_op | source)
XLA Modules:
  0.0 297.5 jit_solution(13894136112145120838)
XLA Ops:
  0.0 5.0 %copy.11 = bf16[8,192,768]{1,0,2:T(8,128)(2,1)} copy(bf16[8,192,768]{2,1,0:T(8,128)(2,1)} %param.3) | data formatting | bytes 4718592 | tf_op args[0]
  5.0 44.4 %all_to_all.41 = bf16[8,192,768]{1,0,2:T(8,128)(2,1)S(1)} all-to-all(bf16[8,192,768]{1,0,2:T(8,128)(2,1)} %copy.11), channel_id=1, replica_groups=mesh['occ'=16,'aux'=16] {'aux'}, dimensions={2} | all-to-all | bytes 4718592 | tf_op jit(solution)/shard_map/all_to_all | solution.py:21
  49.4 0.6 copy.12
  50.1 0.1 copy.13
  50.2 1.1 slice.7
  51.3 1.3 collective-permute-start.1
  52.6 5.5 %collective-permute-start = (bf16[1,3072,48]{1,2,0:T(8,128)(2,1)}, bf16[1,3072,48]{1,2,0:T(8,128)(2,1)S(1)}, u32[]{:S(2)}, u32[]{:S(2)}) collective-permute-start(bf16[1,3072,48]{1,2,0:T(8,128)(2,1)} %slice.7), channel_id=1, source_target_pairs={{0,16},{16,32},{32,48},{48,64},{64,80},{80,96},{96,112},{112,128},... | collective-permute-start | bytes 884744 | tf_op jit(solution)/shard_map/ppermute | solution.py:11
  58.1 3.9 %collective-permute-done.1 = bf16[1,3072,48]{1,2,0:T(8,128)(2,1)S(1)} collective-permute-done((bf16[1,3072,48]{1,2,0:T(8,128)(2,1)}, bf16[1,3072,48]{1,2,0:T(8,128)(2,1)S(1)}, u32[]{:S(2)}, u32[]{:S(2)}) %collective-permute-start.1) | collective-permute-done | bytes 294944 | tf_op jit(solution)/shard_map/ppermute | solution.py:11
  62.0 8.0 %collective-permute-done = bf16[1,3072,48]{1,2,0:T(8,128)(2,1)S(1)} collective-permute-done((bf16[1,3072,48]{1,2,0:T(8,128)(2,1)}, bf16[1,3072,48]{1,2,0:T(8,128)(2,1)S(1)}, u32[]{:S(2)}, u32[]{:S(2)}) %collective-permute-start) | collective-permute-done | bytes 294944 | tf_op jit(solution)/shard_map/ppermute | solution.py:11
  70.1 0.1 pad_maximum_fusion
  70.1 4.8 %stack.4 = bf16[16,2,3072,48]{2,3,1,0:T(8,128)(2,1)} broadcast(bf16[2,3072,48]{1,2,0:T(8,128)(2,1)S(1)} %pad_maximum_fusion), dimensions={1,2,3} | broadcast | bytes 10027008 | tf_op jit(solution)/shard_map/stack | solution.py:33
  75.0 0.0 copy-start.2
  75.0 0.0 copy-start.1
  75.0 5.1 %all-to-all-start.1 = ((bf16[16,2,3072,48]{2,3,1,0:T(8,128)(2,1)}), bf16[16,2,3072,48]{2,3,1,0:T(8,128)(2,1)}, u32[]{:S(2)}, u32[]{:S(2)}) async-start(bf16[16,2,3072,48]{2,3,1,0:T(8,128)(2,1)} %stack.4), calls=%async_computation.1 | async-start | bytes 18874368 | tf_op jit(solution)/shard_map/all_to_all | solution.py:32
  80.1 0.0 copy-done.2
  80.1 0.1 dynamic_slice.13
  80.2 0.0 copy-done.1
  80.2 0.1 dynamic_slice.12
  80.3 0.7 fusion.6
  80.9 1.4 pad_maximum_fusion.1
  82.3 0.1 broadcast_add_fusion
  82.4 1.2 broadcast_subtract_fusion
  83.6 3.4 %copy.15 = bf16[8,16,192,48]{2,1,3,0:T(8,128)(2,1)} copy(bf16[8,16,192,48]{2,0,3,1:T(8,128)(2,1)S(1)} %bitcast.43) | data formatting | bytes 4718592 | tf_op jit(solution)/shard_map/all_to_all | solution.py:21
  87.0 5.1 %reshape.51 = bf16[8,3072,48,1]{1,2,0,3:T(8,128)(2,1)S(1)} reshape(bf16[8,16,192,48]{2,1,3,0:T(8,128)(2,1)} %copy.15) | data formatting | bytes 4718592 | tf_op jit(solution)/shard_map/all_to_all | solution.py:21
  92.1 114.1 %all-to-all-done.1 = bf16[16,2,3072,48]{2,3,1,0:T(8,128)(2,1)} async-done(((bf16[16,2,3072,48]{2,3,1,0:T(8,128)(2,1)}), bf16[16,2,3072,48]{2,3,1,0:T(8,128)(2,1)}, u32[]{:S(2)}, u32[]{:S(2)}) %all-to-all-start.1) | async-done | bytes 9437216 | tf_op jit(solution)/shard_map/all_to_all | solution.py:32
  206.2 8.7 %copy.14 = bf16[16,2,3072,48]{2,3,0,1:T(8,128)(2,1)} copy(bf16[16,2,3072,48]{2,3,1,0:T(8,128)(2,1)} %all-to-all-done.1) | data formatting | bytes 18874368 | tf_op jit(solution)/shard_map/all_to_all | solution.py:32
  214.9 0.0 copy-start
  214.9 8.0 %fusion.1 = bf16[8,48,2,768]{3,1,2,0:T(8,128)(2,1)S(1)} fusion(bf16[2,3072,768,1]{1,2,0,3:T(8,128)(2,1)} %bitcast.47, bf16[8,3072,48,1]{1,2,0,3:T(8,128)(2,1)S(1)} %reshape.51, f32[2]{0:T(128)S(1)} %pad_maximum_fusion.1, f32[8,48,768]{2,1,0:T(8,128)} %broadcast_subtract_fusion), kind=kOutput, calls=%fused_computation.3 | convolution fusion | flops 3625648128 | bytes 14155784 | tf_op jit(solution)/shard_map/iPa,pPb->iapb/dot_general | solution.py:40
  222.9 0.0 copy-done
  222.9 4.2 %fusion = bf16[8,3072,48]{1,2,0:T(8,128)(2,1)S(1)} fusion(bf16[2,3072,768,1]{1,2,0,3:T(8,128)(2,1)S(1)} %bitcast.48, bf16[8,48,2,768]{3,1,2,0:T(8,128)(2,1)S(1)} %fusion.1), kind=kOutput, calls=%fused_computation.1 | convolution fusion | flops 3625058304 | bytes 12976128 | tf_op jit(solution)/shard_map/iapb,pPb->iPa/dot_general | solution.py:48
  227.1 6.0 %copy.18 = bf16[8,3072,48]{2,0,1:T(8,128)(2,1)} copy(bf16[8,3072,48]{1,2,0:T(8,128)(2,1)S(1)} %fusion) | data formatting | bytes 4718592 | tf_op jit(solution)/shard_map/convert_element_type | solution.py:49
  233.1 10.3 %reshape.55 = bf16[16,2,36864]{2,1,0:T(2,128)(2,1)S(1)} reshape(bf16[3072,8,48]{2,1,0:T(8,128)(2,1)} %bitcast.45) | data formatting | bytes 4718592
  243.4 35.0 %all_to_all.42 = bf16[16,2,36864]{2,1,0:T(2,128)(2,1)} all-to-all(bf16[16,2,36864]{2,1,0:T(2,128)(2,1)S(1)} %reshape.55), channel_id=1, replica_groups=mesh['occ'=16,'aux'=16] {'aux'}, dimensions={0} | all-to-all | bytes 4718592 | tf_op jit(solution)/shard_map/all_to_all | solution.py:50
  278.4 9.2 %reshape.56 = bf16[3072,8,48]{2,1,0:T(8,128)(2,1)} reshape(bf16[16,2,36864]{2,1,0:T(2,128)(2,1)} %all_to_all.42) | data formatting | bytes 4718592
  287.7 7.2 %copy.19 = bf16[8,16,192,48]{2,3,1,0:T(8,128)(2,1)S(1)} copy(bf16[8,16,192,48]{3,0,2,1:T(8,128)(2,1)} %bitcast.44) | data formatting | bytes 4718592 | tf_op jit(solution)/shard_map/all_to_all | solution.py:50
  294.9 2.6 copy.20
  (1 shorter events, 0.0 us)
Async XLA Ops:
  51.3 10.7 %collective-permute-start.1 = (bf16[1,3072,48]{1,2,0:T(8,128)(2,1)}, bf16[1,3072,48]{1,2,0:T(8,128)(2,1)S(1)}, u32[]{:S(2)}, u32[]{:S(2)}) collective-permute-start(bf16[1,3072,48]{1,2,0:T(8,128)(2,1)} %slice.7), channel_id=1, source_target_pairs={{16,0},{32,16},{48,32},{64,48},{80,64},{96,80},{112,96},{128,112},... | collective-permute-start | bytes 884744 | tf_op jit(solution)/shard_map/ppermute | solution.py:11
  52.6 17.5 %collective-permute-start = (bf16[1,3072,48]{1,2,0:T(8,128)(2,1)}, bf16[1,3072,48]{1,2,0:T(8,128)(2,1)S(1)}, u32[]{:S(2)}, u32[]{:S(2)}) collective-permute-start(bf16[1,3072,48]{1,2,0:T(8,128)(2,1)} %slice.7), channel_id=1, source_target_pairs={{0,16},{16,32},{32,48},{48,64},{64,80},{80,96},{96,112},{112,128},... | collective-permute-start | bytes 884744 | tf_op jit(solution)/shard_map/ppermute | solution.py:11
  75.0 5.1 %copy-start.2 = (f32[128]{0:T(128)S(1)}, f32[128]{0:T(128)}, u32[]{:S(2)}) copy-start(f32[128]{0:T(128)} %param.4) | copy-start | bytes 1540
  75.0 5.2 %copy-start.1 = (f32[768]{0:T(1024)S(1)}, f32[768]{0:T(1024)}, u32[]{:S(2)}) copy-start(f32[768]{0:T(1024)} %param.5) | copy-start | bytes 9220
  75.0 131.2 %all-to-all-start.1 = ((bf16[16,2,3072,48]{2,3,1,0:T(8,128)(2,1)}), bf16[16,2,3072,48]{2,3,1,0:T(8,128)(2,1)}, u32[]{:S(2)}, u32[]{:S(2)}) async-start(bf16[16,2,3072,48]{2,3,1,0:T(8,128)(2,1)} %stack.4), calls=%async_computation.1 | async-start | bytes 18874368 | tf_op jit(solution)/shard_map/all_to_all | solution.py:32
  214.9 8.0 %copy-start = (bf16[16,2,3072,48]{2,3,0,1:T(8,128)(2,1)S(1)}, bf16[16,2,3072,48]{2,3,0,1:T(8,128)(2,1)}, u32[]{:S(2)}) copy-start(bf16[16,2,3072,48]{2,3,0,1:T(8,128)(2,1)} %copy.14) | copy-start | bytes 28311556
